TPU v7x, 256 devices: a whole 4x4x8 slice. The times are simulated.
256 devices in a mesh: seq: 32 (over z, x), kvh: 8 (over y, core).
Axes of the slice: x: 4, y: 4, z: 8, core: 2. Of those that a mesh axis runs over, the one named last changes fastest.
Arguments:
- queries: bfloat16 [32768, 4096], P('seq', 'kvh'), may hold values from -12 to 12
- kv_cache: bfloat16 [2, 262144, 1024], P(None, 'seq', 'kvh'), may hold values from -6 to 6
- selected: int32 [256, 8, 2], P('seq', 'kvh'), may hold values from 0 to 254, as said below
- out_weight: bfloat16 [4096, 4096], P('kvh', 'seq'), may hold values from -0.125 to 0.125
Outputs:
- output: bfloat16 [32768, 4096], P('seq', 'kvh')
Inputs may be any that keep to these rules, and one draw needn't show every extreme that they name: `selected`: for each KV head, the 16 blocks named by the tiles of one device of seq lie in the ranges of distinct devices (block b lies in the range of device b // 8); for each KV head, some device's range is named by a tile of every device.
All inputs are finite; a program needn't handle non-finite values.
Results may differ from a plain program's by a relative error of at most 0.017.
Values may be sent and summed in bfloat16 or wider, within the bound.
A program may use at most 128 MiB of HBM per device.

v0:
```python
import jax
import jax.numpy as jnp
from jax import lax
from jax.sharding import PartitionSpec as P

GROUP = 4
HD = 128
BLK = 1024
TILE = 128
SEL = 2


def shortened(value):

    def short(part):
        return part.astype(jnp.bfloat16) if part.dtype == jnp.float32 else part

    return jax.tree.map(short, value)


def attend(query_tile, key_rows, value_rows, visible):
    scores = jnp.einsum(
        "igd,kd->gik", query_tile, key_rows, preferred_element_type=jnp.float32
    ) * HD ** (-0.5)
    scores = jnp.where(visible[None], scores, -jnp.inf)
    row_max = jnp.max(scores, axis=2)
    weights = jnp.exp(scores - row_max[:, :, None])
    row_sum = jnp.sum(weights, axis=2)
    summed = jnp.einsum(
        "gik,kd->gid", weights.astype(jnp.bfloat16), value_rows, preferred_element_type=jnp.float32
    )
    return (row_max, row_sum, (summed / row_sum[:, :, None]).astype(jnp.bfloat16))


def combine(row_maxes, row_sums, normeds):
    highest = row_maxes[0]
    for extra in row_maxes[1:]:
        highest = jnp.maximum(highest, extra)
    norm_sum = jnp.zeros_like(highest)
    blended = jnp.zeros(normeds[0].shape, jnp.float32)
    for top_value, sum_value, normed in zip(row_maxes, row_sums, normeds):
        factor = jnp.exp(top_value - highest) * sum_value
        norm_sum = norm_sum + factor
        blended = blended + factor[..., None] * normed.astype(jnp.float32)
    return blended / norm_sum[..., None]


def per_device(queries, kv_cache, selected, out_weight):
    seq_count = lax.axis_size("seq")
    device = lax.axis_index("seq")
    query_count = queries.shape[0]
    tiles_dev = query_count // TILE
    blocks = kv_cache.shape[1] // BLK
    requests = tiles_dev * SEL
    own_block = device * blocks + blocks - 1
    kv_blocks = kv_cache.reshape(2, blocks, BLK, HD)
    query_tiles = queries.reshape(tiles_dev, TILE, GROUP, HD)
    chosen = selected.reshape(requests)
    target = jnp.where(chosen >= own_block, chosen + 1, chosen)
    holder = target // blocks
    within = target % blocks
    request_tile = jnp.arange(requests, dtype=jnp.int32) // SEL
    peers = jnp.arange(seq_count, dtype=jnp.int32)
    routing = holder[None, :] == peers[:, None]
    filled = jnp.any(routing, axis=1).astype(jnp.int32)
    slot_block = jnp.sum(jnp.where(routing, within[None, :], 0), axis=1)
    slot_info = jnp.stack([filled, slot_block], axis=1)
    full_view = jnp.ones((TILE, BLK), dtype=bool)
    key_offsets = jnp.arange(BLK)

    def own_piece(tile_index):
        query_offsets = BLK - query_count + tile_index * TILE + jnp.arange(TILE)
        causal = key_offsets[None, :] <= query_offsets[:, None]
        return attend(
            query_tiles[tile_index], kv_blocks[0, blocks - 1], kv_blocks[1, blocks - 1], causal
        )

    own_max, own_sum, own_out = lax.map(own_piece, jnp.arange(tiles_dev, dtype=jnp.int32))
    slot_tile = jnp.sum(jnp.where(routing, request_tile[None, :], 0), axis=1)
    picking = (slot_tile[:, None] == jnp.arange(tiles_dev)[None, :]) & (filled[:, None] > 0)
    outgoing = jnp.dot(
        picking.astype(jnp.bfloat16),
        queries.reshape(tiles_dev, TILE * GROUP * HD),
        preferred_element_type=jnp.float32,
    )
    outgoing = outgoing.astype(jnp.bfloat16).reshape(seq_count, TILE, GROUP * HD)
    arrived, arrived_info = (
        lax.all_to_all(outgoing, "seq", split_axis=0, concat_axis=0, tiled=True),
        lax.all_to_all(slot_info, "seq", split_axis=0, concat_axis=0, tiled=True),
    )

    def serve(item):
        query_block, info = item
        query_tile = query_block.reshape(TILE, GROUP, HD)

        def work(unused):
            return attend(query_tile, kv_blocks[0, info[1]], kv_blocks[1, info[1]], full_view)

        def skip(unused):
            blank = jnp.zeros((GROUP, TILE), jnp.float32)
            return (blank, blank + 1.0, jnp.zeros((GROUP, TILE, HD), jnp.bfloat16))

        return lax.cond(info[0] > 0, work, skip, 0)

    part_max, part_sum, part_out = lax.map(serve, (arrived, arrived_info))
    back_out = jax.tree.map(
        lambda part, own: part.astype(own.dtype),
        lax.all_to_all(shortened(part_out), "seq", split_axis=0, concat_axis=0, tiled=True),
        part_out,
    )
    back_max, back_sum = (
        lax.all_to_all(part_max, "seq", split_axis=0, concat_axis=0, tiled=True),
        lax.all_to_all(part_sum, "seq", split_axis=0, concat_axis=0, tiled=True),
    )
    picked_max = jnp.take(back_max, holder, axis=0)
    picked_sum = jnp.take(back_sum, holder, axis=0)
    picked_out = jnp.take(back_out, holder, axis=0)
    picked_max = picked_max.reshape(tiles_dev, SEL, GROUP, TILE)
    picked_sum = picked_sum.reshape(tiles_dev, SEL, GROUP, TILE)
    picked_out = picked_out.reshape(tiles_dev, SEL, GROUP, TILE, HD)
    maxima = [own_max] + [picked_max[:, pick] for pick in range(SEL)]
    sums = [own_sum] + [picked_sum[:, pick] for pick in range(SEL)]
    outs = [own_out] + [picked_out[:, pick] for pick in range(SEL)]
    blended = combine(maxima, sums, outs)
    attention = (
        jnp.transpose(blended, (0, 2, 1, 3)).reshape(query_count, GROUP * HD).astype(jnp.bfloat16)
    )
    column_terms = jnp.dot(
        attention,
        lax.all_gather(out_weight, "seq", axis=1, tiled=True),
        preferred_element_type=jnp.float32,
    )
    return lax.psum_scatter(
        column_terms.astype(jnp.bfloat16), "kvh", scatter_dimension=1, tiled=True
    )


def solution(mesh):
    in_specs = (P("seq", "kvh"), P(None, "seq", "kvh"), P("seq", "kvh", None), P("kvh", "seq"))
    out_specs = P("seq", "kvh")
    return jax.shard_map(
        per_device, mesh=mesh, in_specs=in_specs, out_specs=out_specs, check_vma=False
    )
```

profile of v0, /device:TPU:1, one launch (start us, length us, event | category | flops | bytes accessed | tf_op | source)
XLA Modules:
  0.0 686.0 jit_solution(9044395254634991480)
XLA Ops:
  8.3 11.9 %all-to-all-start = ((s32[32,1,2]{2,1,0:T(1,128)}), s32[32,1,2]{2,1,0:T(1,128)S(1)}, u32[]{:S(2)}, u32[]{:S(2)}) async-start(s32[32,1,2]{2,1,0:T(1,128)} %copy.83), calls=%async_computation | async-start | bytes 32768 | tf_op jit(solution)/shard_map/all_to_all | solution.py:89
  23.2 3.5 copy.117
  26.6 6.4 copy.85
  33.1 9.5 %all-to-all-start.1 = ((bf16[32,128,512]{1,2,0:T(8,128)(2,1)}), bf16[32,128,512]{1,2,0:T(8,128)(2,1)}, u32[]{:S(2)}, u32[]{:S(2)}) async-start(bf16[32,128,512]{1,2,0:T(8,128)(2,1)} %copy.85), calls=%async_computation.1 | async-start | bytes 8388608 | tf_op jit(solution)/shard_map/all_to_all | solution.py:88
  43.4 98.6 %all-to-all-done.1 = bf16[32,128,512]{1,2,0:T(8,128)(2,1)} async-done(((bf16[32,128,512]{1,2,0:T(8,128)(2,1)}), bf16[32,128,512]{1,2,0:T(8,128)(2,1)}, u32[]{:S(2)}, u32[]{:S(2)}) %all-to-all-start.1) | async-done | bytes 4194336 | tf_op jit(solution)/shard_map/all_to_all | solution.py:88
  142.0 304.5 %while.29 = (s32[]{:T(128)}, f32[32,4,128]{2,1,0:T(4,128)}, f32[32,4,128]{2,1,0:T(4,128)}, bf16[32,4,128,128]{3,2,1,0:T(8,128)(2,1)}, s32[32,2]{1,0:T(8,128)S(1)...) while((s32[]{:T(128)}, f32[32,4,128]{2,1,0:T(4,128)}, ...), condition=%wide.region_12.13_spmd, body=%wide.region_7.12_spmd.sunk | while | flops 272759808 | bytes 7621869 | solution.py:105
  145.2 8.4 %conditional.2 = (f32[1,4,128]{2,1,0:T(4,128)}, f32[1,4,128]{2,1,0:T(4,128)}, bf16[1,4,128,128]{3,2,1,0:T(8,128)(2,1)S(1)}) conditional(s32[]{:T(128)} %bitcast.143, () %tuple.78, (s32[1,2]{1,0:T(1,128)S(1)}, bf16[2,8,1024,128]{3,2,1,0:T(8,128)(2,1)}, bf16[32,128,512]{1,2,0:T(8,128)(2,1)}, s32[]{:T(128)}) %tuple.79), branch_computations={%region_8.8_spmd, %region_9.11_spmd} | conditional | flops 272759808 | bytes 7350350 | solution.py:103
  155.6 8.4 %conditional.2 = (f32[1,4,128]{2,1,0:T(4,128)}, f32[1,4,128]{2,1,0:T(4,128)}, bf16[1,4,128,128]{3,2,1,0:T(8,128)(2,1)S(1)}) conditional(s32[]{:T(128)} %bitcast.143, () %tuple.78, (s32[1,2]{1,0:T(1,128)S(1)}, bf16[2,8,1024,128]{3,2,1,0:T(8,128)(2,1)}, bf16[32,128,512]{1,2,0:T(8,128)(2,1)}, s32[]{:T(128)}) %tuple.79), branch_computations={%region_8.8_spmd, %region_9.11_spmd} | conditional | flops 272759808 | bytes 7350350 | solution.py:103
  166.0 8.4 %conditional.2 = (f32[1,4,128]{2,1,0:T(4,128)}, f32[1,4,128]{2,1,0:T(4,128)}, bf16[1,4,128,128]{3,2,1,0:T(8,128)(2,1)S(1)}) conditional(s32[]{:T(128)} %bitcast.143, () %tuple.78, (s32[1,2]{1,0:T(1,128)S(1)}, bf16[2,8,1024,128]{3,2,1,0:T(8,128)(2,1)}, bf16[32,128,512]{1,2,0:T(8,128)(2,1)}, s32[]{:T(128)}) %tuple.79), branch_computations={%region_8.8_spmd, %region_9.11_spmd} | conditional | flops 272759808 | bytes 7350350 | solution.py:103
  176.5 8.4 %conditional.2 = (f32[1,4,128]{2,1,0:T(4,128)}, f32[1,4,128]{2,1,0:T(4,128)}, bf16[1,4,128,128]{3,2,1,0:T(8,128)(2,1)S(1)}) conditional(s32[]{:T(128)} %bitcast.143, () %tuple.78, (s32[1,2]{1,0:T(1,128)S(1)}, bf16[2,8,1024,128]{3,2,1,0:T(8,128)(2,1)}, bf16[32,128,512]{1,2,0:T(8,128)(2,1)}, s32[]{:T(128)}) %tuple.79), branch_computations={%region_8.8_spmd, %region_9.11_spmd} | conditional | flops 272759808 | bytes 7350350 | solution.py:103
  186.9 8.4 %conditional.2 = (f32[1,4,128]{2,1,0:T(4,128)}, f32[1,4,128]{2,1,0:T(4,128)}, bf16[1,4,128,128]{3,2,1,0:T(8,128)(2,1)S(1)}) conditional(s32[]{:T(128)} %bitcast.143, () %tuple.78, (s32[1,2]{1,0:T(1,128)S(1)}, bf16[2,8,1024,128]{3,2,1,0:T(8,128)(2,1)}, bf16[32,128,512]{1,2,0:T(8,128)(2,1)}, s32[]{:T(128)}) %tuple.79), branch_computations={%region_8.8_spmd, %region_9.11_spmd} | conditional | flops 272759808 | bytes 7350350 | solution.py:103
  197.3 8.4 %conditional.2 = (f32[1,4,128]{2,1,0:T(4,128)}, f32[1,4,128]{2,1,0:T(4,128)}, bf16[1,4,128,128]{3,2,1,0:T(8,128)(2,1)S(1)}) conditional(s32[]{:T(128)} %bitcast.143, () %tuple.78, (s32[1,2]{1,0:T(1,128)S(1)}, bf16[2,8,1024,128]{3,2,1,0:T(8,128)(2,1)}, bf16[32,128,512]{1,2,0:T(8,128)(2,1)}, s32[]{:T(128)}) %tuple.79), branch_computations={%region_8.8_spmd, %region_9.11_spmd} | conditional | flops 272759808 | bytes 7350350 | solution.py:103
  207.7 8.4 %conditional.2 = (f32[1,4,128]{2,1,0:T(4,128)}, f32[1,4,128]{2,1,0:T(4,128)}, bf16[1,4,128,128]{3,2,1,0:T(8,128)(2,1)S(1)}) conditional(s32[]{:T(128)} %bitcast.143, () %tuple.78, (s32[1,2]{1,0:T(1,128)S(1)}, bf16[2,8,1024,128]{3,2,1,0:T(8,128)(2,1)}, bf16[32,128,512]{1,2,0:T(8,128)(2,1)}, s32[]{:T(128)}) %tuple.79), branch_computations={%region_8.8_spmd, %region_9.11_spmd} | conditional | flops 272759808 | bytes 7350350 | solution.py:103
  218.1 8.4 %conditional.2 = (f32[1,4,128]{2,1,0:T(4,128)}, f32[1,4,128]{2,1,0:T(4,128)}, bf16[1,4,128,128]{3,2,1,0:T(8,128)(2,1)S(1)}) conditional(s32[]{:T(128)} %bitcast.143, () %tuple.78, (s32[1,2]{1,0:T(1,128)S(1)}, bf16[2,8,1024,128]{3,2,1,0:T(8,128)(2,1)}, bf16[32,128,512]{1,2,0:T(8,128)(2,1)}, s32[]{:T(128)}) %tuple.79), branch_computations={%region_8.8_spmd, %region_9.11_spmd} | conditional | flops 272759808 | bytes 7350350 | solution.py:103
  221.6 2.0 bitcast_reduce_fusion
  228.6 8.4 %conditional.2 = (f32[1,4,128]{2,1,0:T(4,128)}, f32[1,4,128]{2,1,0:T(4,128)}, bf16[1,4,128,128]{3,2,1,0:T(8,128)(2,1)S(1)}) conditional(s32[]{:T(128)} %bitcast.143, () %tuple.78, (s32[1,2]{1,0:T(1,128)S(1)}, bf16[2,8,1024,128]{3,2,1,0:T(8,128)(2,1)}, bf16[32,128,512]{1,2,0:T(8,128)(2,1)}, s32[]{:T(128)}) %tuple.79), branch_computations={%region_8.8_spmd, %region_9.11_spmd} | conditional | flops 272759808 | bytes 7350350 | solution.py:103
  239.0 8.4 %conditional.2 = (f32[1,4,128]{2,1,0:T(4,128)}, f32[1,4,128]{2,1,0:T(4,128)}, bf16[1,4,128,128]{3,2,1,0:T(8,128)(2,1)S(1)}) conditional(s32[]{:T(128)} %bitcast.143, () %tuple.78, (s32[1,2]{1,0:T(1,128)S(1)}, bf16[2,8,1024,128]{3,2,1,0:T(8,128)(2,1)}, bf16[32,128,512]{1,2,0:T(8,128)(2,1)}, s32[]{:T(128)}) %tuple.79), branch_computations={%region_8.8_spmd, %region_9.11_spmd} | conditional | flops 272759808 | bytes 7350350 | solution.py:103
  249.4 8.4 %conditional.2 = (f32[1,4,128]{2,1,0:T(4,128)}, f32[1,4,128]{2,1,0:T(4,128)}, bf16[1,4,128,128]{3,2,1,0:T(8,128)(2,1)S(1)}) conditional(s32[]{:T(128)} %bitcast.143, () %tuple.78, (s32[1,2]{1,0:T(1,128)S(1)}, bf16[2,8,1024,128]{3,2,1,0:T(8,128)(2,1)}, bf16[32,128,512]{1,2,0:T(8,128)(2,1)}, s32[]{:T(128)}) %tuple.79), branch_computations={%region_8.8_spmd, %region_9.11_spmd} | conditional | flops 272759808 | bytes 7350350 | solution.py:103
  259.9 8.4 %conditional.2 = (f32[1,4,128]{2,1,0:T(4,128)}, f32[1,4,128]{2,1,0:T(4,128)}, bf16[1,4,128,128]{3,2,1,0:T(8,128)(2,1)S(1)}) conditional(s32[]{:T(128)} %bitcast.143, () %tuple.78, (s32[1,2]{1,0:T(1,128)S(1)}, bf16[2,8,1024,128]{3,2,1,0:T(8,128)(2,1)}, bf16[32,128,512]{1,2,0:T(8,128)(2,1)}, s32[]{:T(128)}) %tuple.79), branch_computations={%region_8.8_spmd, %region_9.11_spmd} | conditional | flops 272759808 | bytes 7350350 | solution.py:103
  270.3 8.4 %conditional.2 = (f32[1,4,128]{2,1,0:T(4,128)}, f32[1,4,128]{2,1,0:T(4,128)}, bf16[1,4,128,128]{3,2,1,0:T(8,128)(2,1)S(1)}) conditional(s32[]{:T(128)} %bitcast.143, () %tuple.78, (s32[1,2]{1,0:T(1,128)S(1)}, bf16[2,8,1024,128]{3,2,1,0:T(8,128)(2,1)}, bf16[32,128,512]{1,2,0:T(8,128)(2,1)}, s32[]{:T(128)}) %tuple.79), branch_computations={%region_8.8_spmd, %region_9.11_spmd} | conditional | flops 272759808 | bytes 7350350 | solution.py:103
  280.8 8.4 %conditional.2 = (f32[1,4,128]{2,1,0:T(4,128)}, f32[1,4,128]{2,1,0:T(4,128)}, bf16[1,4,128,128]{3,2,1,0:T(8,128)(2,1)S(1)}) conditional(s32[]{:T(128)} %bitcast.143, () %tuple.78, (s32[1,2]{1,0:T(1,128)S(1)}, bf16[2,8,1024,128]{3,2,1,0:T(8,128)(2,1)}, bf16[32,128,512]{1,2,0:T(8,128)(2,1)}, s32[]{:T(128)}) %tuple.79), branch_computations={%region_8.8_spmd, %region_9.11_spmd} | conditional | flops 272759808 | bytes 7350350 | solution.py:103
  284.2 2.0 bitcast_reduce_fusion
  291.2 8.4 %conditional.2 = (f32[1,4,128]{2,1,0:T(4,128)}, f32[1,4,128]{2,1,0:T(4,128)}, bf16[1,4,128,128]{3,2,1,0:T(8,128)(2,1)S(1)}) conditional(s32[]{:T(128)} %bitcast.143, () %tuple.78, (s32[1,2]{1,0:T(1,128)S(1)}, bf16[2,8,1024,128]{3,2,1,0:T(8,128)(2,1)}, bf16[32,128,512]{1,2,0:T(8,128)(2,1)}, s32[]{:T(128)}) %tuple.79), branch_computations={%region_8.8_spmd, %region_9.11_spmd} | conditional | flops 272759808 | bytes 7350350 | solution.py:103
  301.6 8.4 %conditional.2 = (f32[1,4,128]{2,1,0:T(4,128)}, f32[1,4,128]{2,1,0:T(4,128)}, bf16[1,4,128,128]{3,2,1,0:T(8,128)(2,1)S(1)}) conditional(s32[]{:T(128)} %bitcast.143, () %tuple.78, (s32[1,2]{1,0:T(1,128)S(1)}, bf16[2,8,1024,128]{3,2,1,0:T(8,128)(2,1)}, bf16[32,128,512]{1,2,0:T(8,128)(2,1)}, s32[]{:T(128)}) %tuple.79), branch_computations={%region_8.8_spmd, %region_9.11_spmd} | conditional | flops 272759808 | bytes 7350350 | solution.py:103
  312.0 8.4 %conditional.2 = (f32[1,4,128]{2,1,0:T(4,128)}, f32[1,4,128]{2,1,0:T(4,128)}, bf16[1,4,128,128]{3,2,1,0:T(8,128)(2,1)S(1)}) conditional(s32[]{:T(128)} %bitcast.143, () %tuple.78, (s32[1,2]{1,0:T(1,128)S(1)}, bf16[2,8,1024,128]{3,2,1,0:T(8,128)(2,1)}, bf16[32,128,512]{1,2,0:T(8,128)(2,1)}, s32[]{:T(128)}) %tuple.79), branch_computations={%region_8.8_spmd, %region_9.11_spmd} | conditional | flops 272759808 | bytes 7350350 | solution.py:103
  322.5 8.4 %conditional.2 = (f32[1,4,128]{2,1,0:T(4,128)}, f32[1,4,128]{2,1,0:T(4,128)}, bf16[1,4,128,128]{3,2,1,0:T(8,128)(2,1)S(1)}) conditional(s32[]{:T(128)} %bitcast.143, () %tuple.78, (s32[1,2]{1,0:T(1,128)S(1)}, bf16[2,8,1024,128]{3,2,1,0:T(8,128)(2,1)}, bf16[32,128,512]{1,2,0:T(8,128)(2,1)}, s32[]{:T(128)}) %tuple.79), branch_computations={%region_8.8_spmd, %region_9.11_spmd} | conditional | flops 272759808 | bytes 7350350 | solution.py:103
  336.0 8.4 %conditional.2 = (f32[1,4,128]{2,1,0:T(4,128)}, f32[1,4,128]{2,1,0:T(4,128)}, bf16[1,4,128,128]{3,2,1,0:T(8,128)(2,1)S(1)}) conditional(s32[]{:T(128)} %bitcast.143, () %tuple.78, (s32[1,2]{1,0:T(1,128)S(1)}, bf16[2,8,1024,128]{3,2,1,0:T(8,128)(2,1)}, bf16[32,128,512]{1,2,0:T(8,128)(2,1)}, s32[]{:T(128)}) %tuple.79), branch_computations={%region_8.8_spmd, %region_9.11_spmd} | conditional | flops 272759808 | bytes 7350350 | solution.py:103
  346.4 8.4 %conditional.2 = (f32[1,4,128]{2,1,0:T(4,128)}, f32[1,4,128]{2,1,0:T(4,128)}, bf16[1,4,128,128]{3,2,1,0:T(8,128)(2,1)S(1)}) conditional(s32[]{:T(128)} %bitcast.143, () %tuple.78, (s32[1,2]{1,0:T(1,128)S(1)}, bf16[2,8,1024,128]{3,2,1,0:T(8,128)(2,1)}, bf16[32,128,512]{1,2,0:T(8,128)(2,1)}, s32[]{:T(128)}) %tuple.79), branch_computations={%region_8.8_spmd, %region_9.11_spmd} | conditional | flops 272759808 | bytes 7350350 | solution.py:103
  356.9 8.4 %conditional.2 = (f32[1,4,128]{2,1,0:T(4,128)}, f32[1,4,128]{2,1,0:T(4,128)}, bf16[1,4,128,128]{3,2,1,0:T(8,128)(2,1)S(1)}) conditional(s32[]{:T(128)} %bitcast.143, () %tuple.78, (s32[1,2]{1,0:T(1,128)S(1)}, bf16[2,8,1024,128]{3,2,1,0:T(8,128)(2,1)}, bf16[32,128,512]{1,2,0:T(8,128)(2,1)}, s32[]{:T(128)}) %tuple.79), branch_computations={%region_8.8_spmd, %region_9.11_spmd} | conditional | flops 272759808 | bytes 7350350 | solution.py:103
  360.3 2.0 bitcast_reduce_fusion
  367.3 8.4 %conditional.2 = (f32[1,4,128]{2,1,0:T(4,128)}, f32[1,4,128]{2,1,0:T(4,128)}, bf16[1,4,128,128]{3,2,1,0:T(8,128)(2,1)S(1)}) conditional(s32[]{:T(128)} %bitcast.143, () %tuple.78, (s32[1,2]{1,0:T(1,128)S(1)}, bf16[2,8,1024,128]{3,2,1,0:T(8,128)(2,1)}, bf16[32,128,512]{1,2,0:T(8,128)(2,1)}, s32[]{:T(128)}) %tuple.79), branch_computations={%region_8.8_spmd, %region_9.11_spmd} | conditional | flops 272759808 | bytes 7350350 | solution.py:103
  377.7 8.4 %conditional.2 = (f32[1,4,128]{2,1,0:T(4,128)}, f32[1,4,128]{2,1,0:T(4,128)}, bf16[1,4,128,128]{3,2,1,0:T(8,128)(2,1)S(1)}) conditional(s32[]{:T(128)} %bitcast.143, () %tuple.78, (s32[1,2]{1,0:T(1,128)S(1)}, bf16[2,8,1024,128]{3,2,1,0:T(8,128)(2,1)}, bf16[32,128,512]{1,2,0:T(8,128)(2,1)}, s32[]{:T(128)}) %tuple.79), branch_computations={%region_8.8_spmd, %region_9.11_spmd} | conditional | flops 272759808 | bytes 7350350 | solution.py:103
  388.1 8.4 %conditional.2 = (f32[1,4,128]{2,1,0:T(4,128)}, f32[1,4,128]{2,1,0:T(4,128)}, bf16[1,4,128,128]{3,2,1,0:T(8,128)(2,1)S(1)}) conditional(s32[]{:T(128)} %bitcast.143, () %tuple.78, (s32[1,2]{1,0:T(1,128)S(1)}, bf16[2,8,1024,128]{3,2,1,0:T(8,128)(2,1)}, bf16[32,128,512]{1,2,0:T(8,128)(2,1)}, s32[]{:T(128)}) %tuple.79), branch_computations={%region_8.8_spmd, %region_9.11_spmd} | conditional | flops 272759808 | bytes 7350350 | solution.py:103
  404.8 8.4 %conditional.2 = (f32[1,4,128]{2,1,0:T(4,128)}, f32[1,4,128]{2,1,0:T(4,128)}, bf16[1,4,128,128]{3,2,1,0:T(8,128)(2,1)S(1)}) conditional(s32[]{:T(128)} %bitcast.143, () %tuple.78, (s32[1,2]{1,0:T(1,128)S(1)}, bf16[2,8,1024,128]{3,2,1,0:T(8,128)(2,1)}, bf16[32,128,512]{1,2,0:T(8,128)(2,1)}, s32[]{:T(128)}) %tuple.79), branch_computations={%region_8.8_spmd, %region_9.11_spmd} | conditional | flops 272759808 | bytes 7350350 | solution.py:103
  415.2 8.4 %conditional.2 = (f32[1,4,128]{2,1,0:T(4,128)}, f32[1,4,128]{2,1,0:T(4,128)}, bf16[1,4,128,128]{3,2,1,0:T(8,128)(2,1)S(1)}) conditional(s32[]{:T(128)} %bitcast.143, () %tuple.78, (s32[1,2]{1,0:T(1,128)S(1)}, bf16[2,8,1024,128]{3,2,1,0:T(8,128)(2,1)}, bf16[32,128,512]{1,2,0:T(8,128)(2,1)}, s32[]{:T(128)}) %tuple.79), branch_computations={%region_8.8_spmd, %region_9.11_spmd} | conditional | flops 272759808 | bytes 7350350 | solution.py:103
  425.6 8.4 %conditional.2 = (f32[1,4,128]{2,1,0:T(4,128)}, f32[1,4,128]{2,1,0:T(4,128)}, bf16[1,4,128,128]{3,2,1,0:T(8,128)(2,1)S(1)}) conditional(s32[]{:T(128)} %bitcast.143, () %tuple.78, (s32[1,2]{1,0:T(1,128)S(1)}, bf16[2,8,1024,128]{3,2,1,0:T(8,128)(2,1)}, bf16[32,128,512]{1,2,0:T(8,128)(2,1)}, s32[]{:T(128)}) %tuple.79), branch_computations={%region_8.8_spmd, %region_9.11_spmd} | conditional | flops 272759808 | bytes 7350350 | solution.py:103
  436.1 8.4 %conditional.2 = (f32[1,4,128]{2,1,0:T(4,128)}, f32[1,4,128]{2,1,0:T(4,128)}, bf16[1,4,128,128]{3,2,1,0:T(8,128)(2,1)S(1)}) conditional(s32[]{:T(128)} %bitcast.143, () %tuple.78, (s32[1,2]{1,0:T(1,128)S(1)}, bf16[2,8,1024,128]{3,2,1,0:T(8,128)(2,1)}, bf16[32,128,512]{1,2,0:T(8,128)(2,1)}, s32[]{:T(128)}) %tuple.79), branch_computations={%region_8.8_spmd, %region_9.11_spmd} | conditional | flops 272759808 | bytes 7350350 | solution.py:103
  446.4 43.0 %all-to-all-start.3 = ((f32[32,4,128]{2,1,0:T(4,128)}), f32[32,4,128]{2,1,0:T(4,128)S(1)}, u32[]{:S(2)}, u32[]{:S(2)}) async-start(f32[32,4,128]{2,1,0:T(4,128)} %get-tuple-element.123), calls=%async_computation.3 | async-start | bytes 131072 | tf_op jit(solution)/shard_map/all_to_all | solution.py:113
  489.4 8.8 %all-to-all-done.3 = f32[32,4,128]{2,1,0:T(4,128)S(1)} async-done(((f32[32,4,128]{2,1,0:T(4,128)}), f32[32,4,128]{2,1,0:T(4,128)S(1)}, u32[]{:S(2)}, u32[]{:S(2)}) %all-to-all-start.3) | async-done | bytes 65568 | tf_op jit(solution)/shard_map/all_to_all | solution.py:113
  498.2 3.9 all-to-all-start.2
  502.5 8.4 %all-to-all-done.2 = f32[32,4,128]{2,1,0:T(4,128)S(1)} async-done(((f32[32,4,128]{2,1,0:T(4,128)}), f32[32,4,128]{2,1,0:T(4,128)S(1)}, u32[]{:S(2)}, u32[]{:S(2)}) %all-to-all-start.2) | async-done | bytes 65568 | tf_op jit(solution)/shard_map/all_to_all | solution.py:112
  511.0 4.9 all-to-all-start.4
  516.1 58.2 %while.30 = (s32[]{:T(128)}, f32[8,4,128]{2,0,1:T(8,128)S(1)}, f32[8,4,128]{2,0,1:T(8,128)S(1)}, bf16[8,4,128,128]{3,2,1,0:T(8,128)(2,1)S(1)}, s32[8]{0:T(128)S(...) while((s32[]{:T(128)}, f32[8,4,128]{2,0,1:T(8,128)S(1)}, ...), condition=%wide.region_3.4_spmd.clone, body=%wide.region_0.3_spmd.clone.sunk | while | flops 274463872 | bytes 7884471 | solution.py:78
  575.7 31.5 %all-to-all-done.4 = bf16[32,4,128,128]{3,2,1,0:T(8,128)(2,1)} async-done(((bf16[32,4,128,128]{3,2,1,0:T(8,128)(2,1)}), bf16[32,4,128,128]{3,2,1,0:T(8,128)(2,1)}, u32[]{:S(2)}, u32[]{:S(2)}) %all-to-all-start.4) | async-done | bytes 4194336 | tf_op jit(solution)/shard_map/all_to_all | solution.py:108
  607.3 3.1 gather_fusion
  610.7 2.5 fusion.42
  613.9 9.0 %convolution_convert_fusion.1 = bf16[1024,4096]{1,0:T(8,128)(2,1)} fusion(bf16[512,4096]{1,0:T(8,128)(2,1)} %all-gather.2.cloned.1.call-done, bf16[64,8,8,128]{3,2,1,0:T(8,128)(2,1)S(1)} %bitcast.158), kind=kOutput, calls=%fused_computation.53 | convolution fusion | flops 4299161600 | bytes 13631488 | tf_op jit(solution)/shard_map/dot_general | solution.py:128
  623.0 56.2 %reduce-scatter.2.cloned.1.call-done = bf16[1024,512]{1,0:T(8,128)(2,1)} async-done(((bf16[1024,4096]{1,0:T(8,128)(2,1)}), bf16[1024,512]{1,0:T(8,128)(2,1)}) %reduce-scatter.2.cloned.1.call-update) | async-done | bytes 1048592 | tf_op jit(solution)/shard_map/reduce_scatter | solution.py:133
  (371 shorter events, 293.1 us)
Async XLA Ops:
  8.3 24.8 %all-to-all-start = ((s32[32,1,2]{2,1,0:T(1,128)}), s32[32,1,2]{2,1,0:T(1,128)S(1)}, u32[]{:S(2)}, u32[]{:S(2)}) async-start(s32[32,1,2]{2,1,0:T(1,128)} %copy.83), calls=%async_computation | async-start | bytes 32768 | tf_op jit(solution)/shard_map/all_to_all | solution.py:89
  33.1 10.3 %copy-start.1 = (s32[8,1,2]{0,2,1:T(2,128)S(1)}, s32[8,1,2]{0,2,1:T(2,128)}, u32[]{:S(2)}) copy-start(s32[8,1,2]{0,2,1:T(2,128)} %param.14) | copy-start | bytes 196
  33.1 108.9 %all-to-all-start.1 = ((bf16[32,128,512]{1,2,0:T(8,128)(2,1)}), bf16[32,128,512]{1,2,0:T(8,128)(2,1)}, u32[]{:S(2)}, u32[]{:S(2)}) async-start(bf16[32,128,512]{1,2,0:T(8,128)(2,1)} %copy.85), calls=%async_computation.1 | async-start | bytes 8388608 | tf_op jit(solution)/shard_map/all_to_all | solution.py:88
  42.5 571.4 %all-gather.2.cloned.1.call-start = ((), (), s32[]{:S(2)}) async-start(), calls=%async_computation.6 | async-start | bytes 4325376 | tf_op jit(solution)/shard_map/all_gather | solution.py:130
  142.0 360.1 %copy-start = (bf16[1024,512]{1,0:T(8,128)(2,1)S(1)}, bf16[1024,512]{1,0:T(8,128)(2,1)}, u32[]{:S(2)}) copy-start(bf16[1024,512]{1,0:T(8,128)(2,1)} %param.12) | copy-start | bytes 3145732
  446.4 51.8 %all-to-all-start.3 = ((f32[32,4,128]{2,1,0:T(4,128)}), f32[32,4,128]{2,1,0:T(4,128)S(1)}, u32[]{:S(2)}, u32[]{:S(2)}) async-start(f32[32,4,128]{2,1,0:T(4,128)} %get-tuple-element.123), calls=%async_computation.3 | async-start | bytes 131072 | tf_op jit(solution)/shard_map/all_to_all | solution.py:113
  498.2 12.7 %all-to-all-start.2 = ((f32[32,4,128]{2,1,0:T(4,128)}), f32[32,4,128]{2,1,0:T(4,128)S(1)}, u32[]{:S(2)}, u32[]{:S(2)}) async-start(f32[32,4,128]{2,1,0:T(4,128)} %get-tuple-element.120), calls=%async_computation.2 | async-start | bytes 131072 | tf_op jit(solution)/shard_map/all_to_all | solution.py:112
  511.0 96.3 %all-to-all-start.4 = ((bf16[32,4,128,128]{3,2,1,0:T(8,128)(2,1)}), bf16[32,4,128,128]{3,2,1,0:T(8,128)(2,1)}, u32[]{:S(2)}, u32[]{:S(2)}) async-start(bf16[32,4,128,128]{3,2,1,0:T(8,128)(2,1)} %get-tuple-element.124), calls=%async_computation.4 | async-start | bytes 8388608 | tf_op jit(solution)/shard_map/all_to_all | solution.py:108
  515.8 163.3 %reduce-scatter.2.cloned.1.call-start = ((), (), s32[]{:S(2)}) async-start(), calls=%async_computation.7 | async-start | bytes 9437184 | tf_op jit(solution)/shard_map/reduce_scatter | solution.py:133
Sparse Core Ops, SparseCore 0:
  45.8 120.8 all-gather.1
  623.1 55.9 reduce-scatter.1
where the time goes:
time: 692 us; the launch traced here: 686 us
  waiting for transfers between devices  204 us (29%)
  local copies, waits for them, and re-layouts  133 us (19%)
  matrix products  132 us (19%)
  loops' own time  76.9 us (11%)
  starting transfers between devices  73.3 us (11%)
  other arithmetic  52.5 us (8%)
  between operations  13.7 us (2%)
    all_to_all x1, waiting for transfers between devices, per_device(): lax.all_to_all(outgoing, 'seq', split_axis=0, concat_axis=0, tiled=True)  98.6 us
    dot_general x36, matrix products, attend(): jnp.einsum('igd,kd->gik', query_tile, key_rows, preferred_element_type=jn...  67.1 us
    dynamic_update_slice x64, local copies, waits for them, and re-layouts, per_device(): part_max, part_sum, part_out = lax.map(serve, (arrived, arrived_info))  61.7 us
    reduce_scatter x1, waiting for transfers between devices, per_device(): lax.psum_scatter(column_terms.astype(jnp.bfloat16), 'kvh', scatter_dimens...  56.2 us
    dot_general x36, matrix products, attend(): jnp.einsum('gik,kd->gid', weights.astype(jnp.bfloat16), value_rows, prefe...  54.6 us
    another operation x32, loops' own time, serve(): return lax.cond(info[0] > 0, work, skip, 0)  54 us
    reduce_sum x36, other arithmetic, attend(): row_sum = jnp.sum(weights, axis=2)  48.2 us
    all_to_all x1, starting transfers between devices, per_device(): lax.all_to_all(part_sum, 'seq', split_axis=0, concat_axis=0, tiled=True)  43 us
  transfers between devices with their start and end apart: 7, of which 5 were waited for; matrix products, arithmetic and copies ran while one was open for 45% of the time, Pallas kernels for 0%

commit v1 on v0

v1 whole, which is shorter than its diff:
```python
import functools

import jax
import jax.numpy as jnp
from jax import lax
from jax.experimental import pallas as pl
from jax.experimental.pallas import tpu as pltpu
from jax.sharding import PartitionSpec as P

GROUP = 4
HD = 128
BLK = 1024
TILE = 128
SEL = 2
ZN = 8
XN = 4
SEQ = ZN * XN
KVN = 8
YN = 4
TILES = 8
BLOCKS = 8
SCALE = HD ** (-0.5)
LOG2E = 1.4426950408889634
MESH = pl.DeviceIdType.MESH
ROUNDS = ((0, 1), (1, 1), (2, 1), (3, 1))


def to_row(column, eye):
    return jnp.sum(jnp.where(eye, column, 0.0), axis=0, keepdims=True)


def to_column(row, eye):
    return jnp.sum(jnp.where(eye, row, 0.0), axis=1, keepdims=True)


def attend(query, keys, values, visible):
    scores = lax.dot_general(
        query, keys, (((1,), (1,)), ((), ())), preferred_element_type=jnp.float32
    )
    if visible is not None:
        scores = jnp.where(visible, scores, -jnp.inf)
    top = jnp.max(scores, axis=1, keepdims=True)
    weights = jnp.exp2((scores - top) * (SCALE * LOG2E))
    total = jnp.sum(weights, axis=1, keepdims=True)
    summed = jnp.dot(
        weights.astype(jnp.bfloat16), values, preferred_element_type=jnp.float32
    )
    return (summed / total).astype(jnp.bfloat16), top * SCALE + jnp.log(total)


def fused(tab, q_ref, kv_ref, blk_ref, w_ref, out_ref, *scratch):
    rounds = len(ROUNDS)
    in_o, in_l, att, own_att = (
        scratch[n * rounds : (n + 1) * rounds] for n in range(4)
    )
    rest = scratch[4 * rounds :]
    out_q, in_q, out_o, out_l, own_o, own_l, in_blk, blk_s, wbuf, wfull, acc = rest[:11]
    q_send, q_recv, b_send, b_recv, o_send, o_recv, l_send, l_recv = rest[11:19]
    a_send, a_recv, s_send, s_recv, z_send, z_recv, x_send, x_recv, local_sem = rest[19:]
    seq = lax.axis_index("seq")
    kvh = lax.axis_index("kvh")
    z, x = seq // XN, seq % XN
    y, core = kvh // 2, kvh % 2

    def ahead(shift):
        return ((z + shift // XN) % ZN) * XN + (x + shift % XN) % XN

    def behind(shift):
        return ((z + ZN - shift // XN) % ZN) * XN + (x + XN - shift % XN) % XN

    def chip(step):
        return ((y + step) % YN) * 2 + core

    sibling = y * 2 + 1 - core

    barrier = pltpu.get_barrier_semaphore()

    def greet_seq(shift, carry):
        pl.semaphore_signal(
            barrier, inc=1, device_id={"seq": ahead(shift)}, device_id_type=MESH
        )
        return carry

    lax.fori_loop(1, SEQ, greet_seq, 0)
    for peer in [chip(1), chip(2), chip(3), sibling]:
        pl.semaphore_signal(barrier, inc=1, device_id={"kvh": peer}, device_id_type=MESH)
    pl.semaphore_wait(barrier, SEQ - 1 + YN)

    def remote(src, dst, send, recv, **device):
        return pltpu.make_async_remote_copy(
            src_ref=src,
            dst_ref=dst,
            send_sem=send,
            recv_sem=recv,
            device_id=device,
            device_id_type=MESH,
        )

    def blk_copy(shift):
        return remote(
            blk_ref.at[shift], in_blk.at[shift], b_send.at[shift], b_recv.at[shift], seq=ahead(shift)
        )

    def q_copy(index, shift):
        first, count = ROUNDS[index]
        heads = pl.ds(first, count)
        return remote(
            out_q.at[shift, heads],
            in_q.at[shift, heads],
            q_send.at[index, shift],
            q_recv.at[index, shift],
            seq=ahead(shift),
        )

    def o_copy(index, shift):
        first, count = ROUNDS[index]
        return remote(
            out_o.at[shift, pl.ds(first, count)],
            in_o[index].at[shift],
            o_send.at[index, shift],
            o_recv.at[index, shift],
            seq=behind(shift),
        )

    def l_copy(index, shift):
        first, count = ROUNDS[index]
        return remote(
            out_l.at[shift, pl.ds(first, count)],
            in_l[index].at[shift],
            l_send.at[index, shift],
            l_recv.at[index, shift],
            seq=behind(shift),
        )

    def lanes(index, head):
        wide = ROUNDS[index][1] * HD
        return pl.ds(pl.multiple_of(head * wide, wide), wide)

    def a_copy(index, step):
        return remote(
            own_att[index],
            att[index].at[:, lanes(index, kvh)],
            a_send.at[index, step],
            a_recv.at[index, step],
            kvh=chip(step),
        )

    def s_copy(index, step):
        part = att[index].at[:, lanes(index, chip(YN - step))]
        return remote(
            own_att[index] if step == 0 else part,
            part,
            s_send.at[index, step],
            s_recv.at[index, step],
            kvh=sibling,
        )

    def z_copy(way, step):
        block = (z + ZN - step + 1) % ZN if way == 0 else (z + step - 1) % ZN
        part = wbuf.at[x, block]
        return remote(
            part,
            part,
            z_send.at[way, step],
            z_recv.at[way, step],
            seq=((z + 1) % ZN if way == 0 else (z + ZN - 1) % ZN) * XN + x,
        )

    def x_copy(step):
        part = wbuf.at[x]
        return remote(
            part, part, x_send.at[step], x_recv.at[step], seq=z * XN + (x + step) % XN
        )

    z_steps = (ZN // 2, ZN // 2 - 1)

    def z_start(step):
        for way in range(2):
            if step <= z_steps[way]:
                z_copy(way, step).start()

    def z_wait(step):
        for way in range(2):
            if step <= z_steps[way]:
                z_copy(way, step).wait_recv()

    eye = lax.broadcasted_iota(jnp.int32, (TILE, TILE), 0) == lax.broadcasted_iota(
        jnp.int32, (TILE, TILE), 1
    )

    def own_piece(tile, carry):
        visible = lax.broadcasted_iota(jnp.int32, (TILE, BLK), 1) <= (
            tile * TILE + lax.broadcasted_iota(jnp.int32, (TILE, BLK), 0)
        )
        for head in range(GROUP):
            out, lse = attend(
                q_ref[tile, :, head * HD : (head + 1) * HD],
                kv_ref[0, BLOCKS - 1],
                kv_ref[1, BLOCKS - 1],
                visible,
            )
            own_o[tile, head] = out
            own_l[tile, head] = to_row(lse, eye)
        return carry

    def send_blk(shift, carry):
        blk_copy(shift).start()
        return carry

    def send_queries(index):
        first, count = ROUNDS[index]

        def pack(shift, carry):
            tile = tab[shift]
            for head in range(first, first + count):
                out_q[shift, head] = q_ref[tile, :, head * HD : (head + 1) * HD]
            q_copy(index, shift).start()
            return carry

        for head in range(first, first + count):
            in_q[0, head] = q_ref[tab[0], :, head * HD : (head + 1) * HD]
        lax.fori_loop(1, SEQ, pack, 0)

    def serve_round(index):
        first, count = ROUNDS[index]

        def serve(shift, home):
            block = blk_s[shift, 0, 0]
            for head in range(first, first + count):
                out, lse = attend(
                    in_q[shift, head], kv_ref[0, block], kv_ref[1, block], None
                )
                if home:
                    in_o[index][shift, head - first] = out
                    in_l[index][shift, head - first] = to_row(lse, eye)
                else:
                    out_o[shift, head] = out
                    out_l[shift, head] = to_row(lse, eye)

        def step(shift, carry):
            q_copy(index, shift).wait_recv()
            serve(shift, False)
            o_copy(index, shift).start()
            l_copy(index, shift).start()
            return carry

        serve(0, True)
        lax.fori_loop(1, SEQ, step, 0)

    def mix_round(index):
        first, count = ROUNDS[index]

        def arrived(shift, carry):
            o_copy(index, shift).wait_recv()
            l_copy(index, shift).wait_recv()
            return carry

        lax.fori_loop(1, SEQ, arrived, 0)

        def mix(tile, carry):
            one = tab[SEQ + tile * SEL]
            two = tab[SEQ + tile * SEL + 1]
            row = pl.multiple_of(tile * TILE, TILE)
            for head in range(first, first + count):
                at = head - first
                rows = [own_l[tile, head], in_l[index][one, at], in_l[index][two, at]]
                outs = [own_o[tile, head], in_o[index][one, at], in_o[index][two, at]]
                high = jnp.maximum(jnp.maximum(rows[0], rows[1]), rows[2])
                parts = [jnp.exp(r - high) for r in rows]
                norm = parts[0] + parts[1] + parts[2]
                blended = jnp.zeros((TILE, HD), jnp.float32)
                for part, out in zip(parts, outs):
                    blended = blended + to_column(part / norm, eye) * out.astype(jnp.float32)
                own_att[index][pl.ds(row, TILE), at * HD : (at + 1) * HD] = blended.astype(
                    jnp.bfloat16
                )
            return carry

        lax.fori_loop(0, TILES, mix, 0)
        for step in range(1, YN):
            a_copy(index, step).start()
        s_copy(index, 0).start()
        keep(index).start()

    def keep(index):
        return pltpu.make_async_copy(
            own_att[index], att[index].at[:, lanes(index, kvh)], local_sem.at[1 + index]
        )

    def pass_on(index):
        for step in range(1, YN):
            a_copy(index, step).wait_recv()
            s_copy(index, step).start()

    def project(index):
        first, count = ROUNDS[index]
        for step in range(YN):
            s_copy(index, step).wait_recv()
        keep(index).wait()
        last = index == rounds - 1

        def rows_of(tile, carry):
            rows = pl.ds(pl.multiple_of(tile * 256, 256), 256)
            term = jnp.dot(
                att[index][rows, :],
                wfull[first * KVN * HD : (first + count) * KVN * HD, :],
                preferred_element_type=jnp.float32,
            )
            if index > 0:
                term = acc[rows, :] + term
            if last:
                out_ref[rows, :] = term.astype(jnp.bfloat16)
            else:
                acc[rows, :] = term
            return carry

        lax.fori_loop(0, TILES // 2, rows_of, 0)

    wbuf[x, z] = w_ref[...]
    z_start(1)
    lax.fori_loop(1, SEQ, send_blk, 0)
    tiles = TILES // rounds
    for index in range(rounds):
        send_queries(index)
        lax.fori_loop(index * tiles, (index + 1) * tiles, own_piece, 0)
        z_wait(index + 1)
        if index + 1 < rounds:
            z_start(index + 2)
    for step in range(1, XN):
        x_copy(step).start()

    def wait_blk(shift, carry):
        blk_copy(shift).wait_recv()
        return carry

    lax.fori_loop(1, SEQ, wait_blk, 0)
    in_blk[0] = blk_ref[0]
    fetch = pltpu.make_async_copy(in_blk, blk_s, local_sem.at[0])
    fetch.start()
    fetch.wait()

    serve_round(0)
    serve_round(1)
    mix_round(0)
    serve_round(2)
    pass_on(0)
    mix_round(1)
    serve_round(3)
    pass_on(1)
    mix_round(2)

    for step in range(1, XN):
        x_copy(step).wait_recv()
    for index, (first, count) in enumerate(ROUNDS):

        def arrange(head, carry, first=first, count=count):
            row = pl.multiple_of((first * KVN + head * count) * HD, HD)
            for col in range(XN):
                wfull[pl.ds(row, count * HD), col * HD : (col + 1) * HD] = wbuf[
                    col, head, first * HD : (first + count) * HD, :
                ]
            return carry

        lax.fori_loop(0, KVN, arrange, 0)

    project(0)
    project(1)
    pass_on(2)
    mix_round(3)
    project(2)
    pass_on(3)
    project(3)

    for index in range(rounds):

        def finish(shift, carry, index=index):
            q_copy(index, shift).wait_send()
            o_copy(index, shift).wait_send()
            l_copy(index, shift).wait_send()
            return carry

        lax.fori_loop(1, SEQ, finish, 0)
        for step in range(1, YN):
            a_copy(index, step).wait_send()
        for step in range(YN):
            s_copy(index, step).wait_send()

    def finish_blk(shift, carry):
        blk_copy(shift).wait_send()
        return carry

    lax.fori_loop(1, SEQ, finish_blk, 0)
    for way in range(2):
        for step in range(1, z_steps[way] + 1):
            z_copy(way, step).wait_send()
    for step in range(1, XN):
        x_copy(step).wait_send()


def per_device(queries, kv_cache, selected, out_weight):
    rows = queries.shape[0]
    seq = lax.axis_index("seq")
    z, x = seq // XN, seq % XN
    moves = []
    for sz in range(ZN):
        for sx in range(XN):
            for k in range(KVN):
                moves.append(((sz * XN + sx) * KVN + k, (k * XN + sx) * KVN + sz))
    moved = lax.ppermute(out_weight, ("seq", "kvh"), moves)

    own_block = seq * BLOCKS + BLOCKS - 1
    chosen = selected.reshape(TILES * SEL)
    target = jnp.where(chosen >= own_block, chosen + 1, chosen)
    holder = target // BLOCKS
    within = target % BLOCKS
    shift = ((holder // XN - z + ZN) % ZN) * XN + (holder % XN - x + XN) % XN
    routing = shift[None, :] == jnp.arange(SEQ, dtype=jnp.int32)[:, None]
    request_tile = jnp.arange(TILES * SEL, dtype=jnp.int32) // SEL
    slot_tile = jnp.sum(jnp.where(routing, request_tile[None, :], 0), axis=1)
    slot_block = jnp.sum(jnp.where(routing, within[None, :], 0), axis=1)
    table = jnp.concatenate([slot_tile, shift]).astype(jnp.int32)
    slot_block = jnp.broadcast_to(slot_block.astype(jnp.int32)[:, None, None], (SEQ, 1, 128))

    rounds = len(ROUNDS)
    vmem = pl.BlockSpec(memory_space=pltpu.VMEM)
    dma = pltpu.SemaphoreType.DMA
    slots = pltpu.VMEM((SEQ, GROUP, TILE, HD), jnp.bfloat16)
    return pl.pallas_call(
        fused,
        name="fused",
        out_shape=jax.ShapeDtypeStruct((rows, XN * HD), jnp.bfloat16),
        in_specs=[pl.BlockSpec(memory_space=pltpu.SMEM), vmem, vmem, vmem, vmem],
        out_specs=vmem,
        scratch_shapes=[pltpu.VMEM((SEQ, n, TILE, HD), jnp.bfloat16) for _, n in ROUNDS]
        + [pltpu.VMEM((SEQ, n, 1, TILE), jnp.float32) for _, n in ROUNDS]
        + [pltpu.VMEM((rows, KVN * n * HD), jnp.bfloat16) for _, n in ROUNDS]
        + [pltpu.VMEM((rows, n * HD), jnp.bfloat16) for _, n in ROUNDS]
        + [
            slots,
            slots,
            slots,
            pltpu.VMEM((SEQ, GROUP, 1, TILE), jnp.float32),
            pltpu.VMEM((TILES, GROUP, TILE, HD), jnp.bfloat16),
            pltpu.VMEM((TILES, GROUP, 1, TILE), jnp.float32),
            pltpu.VMEM((SEQ, 1, 128), jnp.int32),
            pltpu.SMEM((SEQ, 1, 128), jnp.int32),
            pltpu.VMEM((XN, KVN, GROUP * HD, HD), jnp.bfloat16),
            pltpu.VMEM((KVN * GROUP * HD, XN * HD), jnp.bfloat16),
            pltpu.VMEM((rows, XN * HD), jnp.float32),
        ]
        + [dma((rounds, SEQ))] * 2
        + [dma((SEQ,))] * 2
        + [dma((rounds, SEQ))] * 4
        + [dma((rounds, YN))] * 4
        + [dma((2, ZN))] * 2
        + [dma((XN,))] * 2
        + [dma((1 + rounds,))],
        compiler_params=pltpu.CompilerParams(
            collective_id=0, has_side_effects=True, vmem_limit_bytes=60 << 20
        ),
    )(
        table,
        queries.reshape(TILES, TILE, GROUP * HD),
        kv_cache.reshape(2, BLOCKS, BLK, HD),
        slot_block,
        moved,
    )


def solution(mesh):
    in_specs = (P("seq", "kvh"), P(None, "seq", "kvh"), P("seq", "kvh", None), P("kvh", "seq"))
    out_specs = P("seq", "kvh")
    return jax.shard_map(
        per_device, mesh=mesh, in_specs=in_specs, out_specs=out_specs, check_vma=False
    )
```

time: 692 us -> 280 us (0.40)
  Pallas kernels: 0 us -> 270 us
  waiting for transfers between devices: 204 us -> 1.26 us
  matrix products: 132 us -> 0 us
  local copies, waits for them, and re-layouts: 133 us -> 3.8 us
  loops' own time: 76.9 us -> 0 us
  starting transfers between devices: 73.3 us -> 4.92 us
  other arithmetic: 52.5 us -> 0.72 us
  between operations: 13.7 us -> 0.04 us
    pallas_call x0 -> x1, Pallas kernels: none -> 270 us  [per_device(): pl.pallas_call(fused, name='fused', out_shape=jax.ShapeDtypeStruct((rows,...]
    all_to_all x5 -> x0, waiting for transfers between devices: 147 us -> none  [the longest x1 98.6 us: per_device(): lax.all_to_all(outgoing, 'seq', split_axis=0, concat_axis=0, tiled=True)]
    dot_general x74 -> x0, matrix products: 132 us -> none  [the longest x36 67.1 us: attend(): jnp.einsum('igd,kd->gik', query_tile, key_rows, preferred_element_type=jn...]
    another operation x34 -> x0, loops' own time: 76.9 us -> none  [the longest x32 54 us: serve(): return lax.cond(info[0] > 0, work, skip, 0)]
    all_to_all x5 -> x0, starting transfers between devices: 73 us -> none  [the longest x1 43 us: per_device(): lax.all_to_all(part_sum, 'seq', split_axis=0, concat_axis=0, tiled=True)]
    dynamic_update_slice x80 -> x0, local copies, waits for them, and re-layouts: 62.2 us -> none  [the longest x64 61.7 us: per_device(): part_max, part_sum, part_out = lax.map(serve, (arrived, arrived_info))]
    reduce_scatter x1 -> x0, waiting for transfers between devices: 56.2 us -> none  [per_device(): lax.psum_scatter(column_terms.astype(jnp.bfloat16), 'kvh', scatter_dimens...]
    reduce_sum x37 -> x1, other arithmetic: 48.3 us -> 0.09 us  [per_device(): slot_block = jnp.sum(jnp.where(routing, within[None, :], 0), axis=1)]
  transfers between devices with their start and end apart: 7 -> 1, of which waited for: 5 -> 1; matrix products, arithmetic and copies ran while one was open for 45% -> 1% of each run, Pallas kernels for 0% -> 0%
where the time goes in v1:
time: 280 us
  Pallas kernels  270 us (96%)
  starting transfers between devices  4.92 us (2%)
  local copies, waits for them, and re-layouts  3.8 us (1%)
    pallas_call x1, Pallas kernels, per_device(): pl.pallas_call(fused, name='fused', out_shape=jax.ShapeDtypeStruct((rows,...  270 us
  transfers between devices with their start and end apart: 1, of which 1 were waited for; matrix products, arithmetic and copies ran while one was open for 1% of the time, Pallas kernels for 0%

profile of v1, /device:TPU:1, one launch (start us, length us, event | category | flops | bytes accessed | tf_op | source)
XLA Modules:
  0.0 280.3 jit_solution(11131630362826775734)
XLA Ops:
  0.0 4.9 %collective-permute-start = (bf16[512,128]{1,0:T(8,128)(2,1)}, bf16[512,128]{1,0:T(8,128)(2,1)S(1)}, u32[]{:S(2)}, u32[]{:S(2)}) collective-permute-start(bf16[512,128]{1,0:T(8,128)(2,1)} %param.7), channel_id=1, source_target_pairs={{0,0},{1,32},{2,64},{3,96},{4,128},{5,160},{6,192},{7,224},{8,8},{... | collective-permute-start | bytes 393224 | tf_op jit(solution)/shard_map/ppermute | solution.py:409
  4.9 0.8 copy.7
  5.7 0.1 reshape.125
  5.8 0.1 select_reduce_fusion
  5.9 0.6 pad_add_fusion.tab
  6.5 1.3 collective-permute-done.w_ref
  7.8 0.0 copy-start
  7.8 0.7 broadcast_in_dim.31.blk_ref
  8.5 0.0 copy-done
  8.5 269.5 %fused.1 = bf16[1024,512]{1,0:T(8,128)(2,1)} custom-call(s32[48]{0:T(128)} %pad_add_fusion.tab, bf16[8,128,512]{2,1,0:T(8,128)(2,1)} %bitcast.5, bf16[2,8,1024,128]{3,2,1,0:T(8,128)(2,1)} %bitcast.4, s32[32,1,128]{2,1,0:T(1,128)} %broadcast_in_dim.31.blk_ref, bf16[512,128]{1,0:T(8,128)(2,1)} %copy-done), custom_call_target="tpu_custom_call" | custom-call | tf_op jit(solution)/shard_map/fused/pallas_call | solution.py:428
  278.0 2.3 copy.9
  (2 shorter events, 0.0 us)
Async XLA Ops:
  0.0 7.8 %collective-permute-start = (bf16[512,128]{1,0:T(8,128)(2,1)}, bf16[512,128]{1,0:T(8,128)(2,1)S(1)}, u32[]{:S(2)}, u32[]{:S(2)}) collective-permute-start(bf16[512,128]{1,0:T(8,128)(2,1)} %param.7), channel_id=1, source_target_pairs={{0,0},{1,32},{2,64},{3,96},{4,128},{5,160},{6,192},{7,224},{8,8},{... | collective-permute-start | bytes 393224 | tf_op jit(solution)/shard_map/ppermute | solution.py:409
  7.8 0.7 copy-start

commit v2 on v1

--- a/solution.py
+++ b/solution.py
@@ -48,15 +48,15 @@
     return (summed / total).astype(jnp.bfloat16), top * SCALE + jnp.log(total)
 
 
-def fused(tab, q_ref, kv_ref, blk_ref, w_ref, out_ref, *scratch):
+def fused(tab, q_ref, cache_ref, blk_ref, w_ref, out_ref, *scratch):
     rounds = len(ROUNDS)
     in_o, in_l, att, own_att = (
         scratch[n * rounds : (n + 1) * rounds] for n in range(4)
     )
     rest = scratch[4 * rounds :]
-    out_q, in_q, out_o, out_l, own_o, own_l, in_blk, blk_s, wbuf, wfull, acc = rest[:11]
-    q_send, q_recv, b_send, b_recv, o_send, o_recv, l_send, l_recv = rest[11:19]
-    a_send, a_recv, s_send, s_recv, z_send, z_recv, x_send, x_recv, local_sem = rest[19:]
+    out_q, in_q, out_o, out_l, own_o, own_l, in_blk, blk_s, wbuf, wfull, acc, kv_ref = rest[:12]
+    q_send, q_recv, b_send, b_recv, o_send, o_recv, l_send, l_recv = rest[12:20]
+    a_send, a_recv, s_send, s_recv, z_send, z_recv, x_send, x_recv, p_sem, local_sem = rest[20:]
     seq = lax.axis_index("seq")
     kvh = lax.axis_index("kvh")
     z, x = seq // XN, seq % XN
@@ -72,6 +72,8 @@
         return ((y + step) % YN) * 2 + core
 
     sibling = y * 2 + 1 - core
+    cache = pltpu.make_async_copy(cache_ref, kv_ref, local_sem.at[1 + rounds])
+    cache.start()
 
     barrier = pltpu.get_barrier_semaphore()
 
@@ -84,7 +86,16 @@
     lax.fori_loop(1, SEQ, greet_seq, 0)
     for peer in [chip(1), chip(2), chip(3), sibling]:
         pl.semaphore_signal(barrier, inc=1, device_id={"kvh": peer}, device_id_type=MESH)
-    pl.semaphore_wait(barrier, SEQ - 1 + YN)
+    partner = {"seq": kvh * XN + x, "kvh": z}
+
+    @pl.when(kvh != z)
+    def _():
+        pl.semaphore_signal(barrier, inc=1, device_id=partner, device_id_type=MESH)
+        pl.semaphore_wait(barrier, SEQ + YN)
+
+    @pl.when(kvh == z)
+    def _():
+        pl.semaphore_wait(barrier, SEQ - 1 + YN)
 
     def remote(src, dst, send, recv, **device):
         return pltpu.make_async_remote_copy(
@@ -166,11 +177,24 @@
             seq=((z + 1) % ZN if way == 0 else (z + ZN - 1) % ZN) * XN + x,
         )
 
-    def x_copy(step):
-        part = wbuf.at[x]
-        return remote(
-            part, part, x_send.at[step], x_recv.at[step], seq=z * XN + (x + step) % XN
-        )
+    def p_copy():
+        return remote(w_ref, wbuf.at[x, kvh], p_sem.at[0], p_sem.at[1], **partner)
+
+    def x_copy(piece, step):
+        block = (z + ZN - piece) % ZN
+        part = wbuf.at[x, block]
+        return remote(
+            part,
+            part,
+            x_send.at[piece, step],
+            x_recv.at[piece, step],
+            seq=z * XN + (x + step) % XN,
+        )
+
+    def x_start(*pieces):
+        for piece in pieces:
+            for step in (2, 1, 3):
+                x_copy(piece, step).start()
 
     z_steps = (ZN // 2, ZN // 2 - 1)
 
@@ -221,7 +245,7 @@
             in_q[0, head] = q_ref[tab[0], :, head * HD : (head + 1) * HD]
         lax.fori_loop(1, SEQ, pack, 0)
 
-    def serve_round(index):
+    def serve_round(index, between=()):
         first, count = ROUNDS[index]
 
         def serve(shift, home):
@@ -245,7 +269,12 @@
             return carry
 
         serve(0, True)
-        lax.fori_loop(1, SEQ, step, 0)
+        cuts = [1 + (SEQ - 1) * n // (len(between) + 1) for n in range(len(between) + 2)]
+        for number in range(len(cuts) - 1):
+            lax.fori_loop(cuts[number], cuts[number + 1], step, 0)
+            if number < len(between):
+                piece, distance = between[number]
+                x_copy(piece, distance).start()
 
     def mix_round(index):
         first, count = ROUNDS[index]
@@ -316,18 +345,34 @@
 
         lax.fori_loop(0, TILES // 2, rows_of, 0)
 
-    wbuf[x, z] = w_ref[...]
-    z_start(1)
+    @pl.when(kvh != z)
+    def _():
+        p_copy().start()
+
+    @pl.when(kvh == z)
+    def _():
+        wbuf[x, z] = w_ref[...]
+
     lax.fori_loop(1, SEQ, send_blk, 0)
     tiles = TILES // rounds
     for index in range(rounds):
         send_queries(index)
+        if index == 0:
+            cache.wait()
+        if index == 1:
+            x_start(0)
+        if index == 2:
+            x_start(1, 7)
         lax.fori_loop(index * tiles, (index + 1) * tiles, own_piece, 0)
-        z_wait(index + 1)
-        if index + 1 < rounds:
-            z_start(index + 2)
-    for step in range(1, XN):
-        x_copy(step).start()
+        if index == 0:
+
+            @pl.when(kvh != z)
+            def _():
+                p_copy().wait()
+
+        else:
+            z_wait(index)
+        z_start(index + 1)
 
     def wait_blk(shift, carry):
         blk_copy(shift).wait_recv()
@@ -339,18 +384,20 @@
     fetch.start()
     fetch.wait()
 
-    serve_round(0)
-    serve_round(1)
+    serve_round(0, [(p, d) for p in (2, 6) for d in (2, 1, 3)])
+    z_wait(rounds)
+    serve_round(1, [(p, d) for p in (3, 5) for d in (2, 1, 3)])
     mix_round(0)
-    serve_round(2)
+    serve_round(2, [(4, d) for d in (2, 1, 3)])
     pass_on(0)
     mix_round(1)
     serve_round(3)
     pass_on(1)
     mix_round(2)
 
-    for step in range(1, XN):
-        x_copy(step).wait_recv()
+    for piece in range(ZN):
+        for step in range(1, XN):
+            x_copy(piece, step).wait_recv()
     for index, (first, count) in enumerate(ROUNDS):
 
         def arrange(head, carry, first=first, count=count):
@@ -393,21 +440,15 @@
     for way in range(2):
         for step in range(1, z_steps[way] + 1):
             z_copy(way, step).wait_send()
-    for step in range(1, XN):
-        x_copy(step).wait_send()
+    for piece in range(ZN):
+        for step in range(1, XN):
+            x_copy(piece, step).wait_send()
 
 
 def per_device(queries, kv_cache, selected, out_weight):
     rows = queries.shape[0]
     seq = lax.axis_index("seq")
     z, x = seq // XN, seq % XN
-    moves = []
-    for sz in range(ZN):
-        for sx in range(XN):
-            for k in range(KVN):
-                moves.append(((sz * XN + sx) * KVN + k, (k * XN + sx) * KVN + sz))
-    moved = lax.ppermute(out_weight, ("seq", "kvh"), moves)
-
     own_block = seq * BLOCKS + BLOCKS - 1
     chosen = selected.reshape(TILES * SEL)
     target = jnp.where(chosen >= own_block, chosen + 1, chosen)
@@ -429,7 +470,13 @@
         fused,
         name="fused",
         out_shape=jax.ShapeDtypeStruct((rows, XN * HD), jnp.bfloat16),
-        in_specs=[pl.BlockSpec(memory_space=pltpu.SMEM), vmem, vmem, vmem, vmem],
+        in_specs=[
+            pl.BlockSpec(memory_space=pltpu.SMEM),
+            vmem,
+            pl.BlockSpec(memory_space=pl.ANY),
+            vmem,
+            vmem,
+        ],
         out_specs=vmem,
         scratch_shapes=[pltpu.VMEM((SEQ, n, TILE, HD), jnp.bfloat16) for _, n in ROUNDS]
         + [pltpu.VMEM((SEQ, n, 1, TILE), jnp.float32) for _, n in ROUNDS]
@@ -447,14 +494,16 @@
             pltpu.VMEM((XN, KVN, GROUP * HD, HD), jnp.bfloat16),
             pltpu.VMEM((KVN * GROUP * HD, XN * HD), jnp.bfloat16),
             pltpu.VMEM((rows, XN * HD), jnp.float32),
+            pltpu.VMEM((2, BLOCKS, BLK, HD), jnp.bfloat16),
         ]
         + [dma((rounds, SEQ))] * 2
         + [dma((SEQ,))] * 2
         + [dma((rounds, SEQ))] * 4
         + [dma((rounds, YN))] * 4
         + [dma((2, ZN))] * 2
-        + [dma((XN,))] * 2
-        + [dma((1 + rounds,))],
+        + [dma((ZN, XN))] * 2
+        + [dma((2,))]
+        + [dma((2 + rounds,))],
         compiler_params=pltpu.CompilerParams(
             collective_id=0, has_side_effects=True, vmem_limit_bytes=60 << 20
         ),
@@ -463,7 +512,7 @@
         queries.reshape(TILES, TILE, GROUP * HD),
         kv_cache.reshape(2, BLOCKS, BLK, HD),
         slot_block,
-        moved,
+        out_weight,
     )
 
 

time: 280 us -> 248 us (0.89)
  Pallas kernels: 270 us -> 243 us
  starting transfers between devices: 4.92 us -> 0 us
    pallas_call x1, Pallas kernels: 270 us -> 243 us  [per_device(): pl.pallas_call(fused, name='fused', out_shape=jax.ShapeDtypeStruct((rows,...]
    ppermute x1 -> x0, starting transfers between devices: 4.92 us -> none  [per_device(): moved = lax.ppermute(out_weight, ('seq', 'kvh'), moves)]
  transfers between devices with their start and end apart: 1 -> 0, of which waited for: 1 -> 0; matrix products, arithmetic and copies ran while one was open for 1% -> 0% of each run, Pallas kernels for 0% -> 0%
where the time goes in v2:
time: 248 us; the launch traced here: 247 us
  Pallas kernels  243 us (98%)
  local copies, waits for them, and re-layouts  3.8 us (2%)
    pallas_call x1, Pallas kernels, per_device(): pl.pallas_call(fused, name='fused', out_shape=jax.ShapeDtypeStruct((rows,...  243 us

profile of v2, /device:TPU:1, one launch (start us, length us, event | category | flops | bytes accessed | tf_op | source)
XLA Modules:
  0.0 247.1 jit_solution(14158963169219567030)
XLA Ops:
  0.0 0.8 copy.7
  0.8 0.1 reshape.125
  0.9 0.1 select_reduce_fusion
  1.0 0.7 pad_add_fusion.tab
  1.6 0.7 broadcast_in_dim.31.blk_ref
  2.3 242.5 %fused.1 = bf16[1024,512]{1,0:T(8,128)(2,1)} custom-call(s32[48]{0:T(128)} %pad_add_fusion.tab, bf16[8,128,512]{2,1,0:T(8,128)(2,1)} %bitcast.5, bf16[2,8,1024,128]{3,2,1,0:T(8,128)(2,1)} %bitcast.4, s32[32,1,128]{2,1,0:T(1,128)} %broadcast_in_dim.31.blk_ref, bf16[512,128]{1,0:T(8,128)(2,1)} %w_ref.1), custom_call_target="tpu_custom_call" | custom-call | tf_op jit(solution)/shard_map/fused/pallas_call | solution.py:469
  244.9 2.3 copy.9
  (2 shorter events, 0.0 us)

commit v3 on v2

v3 whole, which is shorter than its diff:
```python
import functools

import jax
import jax.numpy as jnp
from jax import lax
from jax.experimental import pallas as pl
from jax.experimental.pallas import tpu as pltpu
from jax.sharding import PartitionSpec as P

GROUP = 4
HD = 128
BLK = 1024
TILE = 128
SEL = 2
ZN = 8
XN = 4
SEQ = ZN * XN
KVN = 8
YN = 4
TILES = 8
BLOCKS = 8
SCALE = HD ** (-0.5)
LOG2E = 1.4426950408889634
MESH = pl.DeviceIdType.MESH
PARTS = ((0, 0, 128), (1, 0, 128), (2, 0, 128), (3, 0, 64), (3, 64, 64))


def to_row(column, eye):
    return jnp.sum(jnp.where(eye, column, 0.0), axis=0, keepdims=True)


def to_column(row, eye):
    return jnp.sum(jnp.where(eye, row, 0.0), axis=1, keepdims=True)


def attend(query, keys, values, visible):
    scores = lax.dot_general(
        query, keys, (((1,), (1,)), ((), ())), preferred_element_type=jnp.float32
    )
    if visible is not None:
        scores = jnp.where(visible, scores, -jnp.inf)
    top = jnp.max(scores, axis=1, keepdims=True)
    weights = jnp.exp2((scores - top) * (SCALE * LOG2E))
    total = jnp.sum(weights, axis=1, keepdims=True)
    summed = jnp.dot(
        weights.astype(jnp.bfloat16), values, preferred_element_type=jnp.float32
    )
    return (summed / total).astype(jnp.bfloat16), top * SCALE + jnp.log(total)


def fused(tab, q_ref, cache_ref, blk_ref, w_ref, out_ref, *scratch):
    parts = len(PARTS)
    in_o, att, own_att = (scratch[n * parts : (n + 1) * parts] for n in range(3))
    in_l, out_l = scratch[3 * parts : 3 * parts + GROUP], scratch[3 * parts + GROUP :][:GROUP]
    rest = scratch[3 * parts + 2 * GROUP :]
    out_q, in_q, out_o, own_o, own_l, in_blk, blk_s, wbuf, wfull, acc, kv_ref = rest[:11]
    q_send, q_recv, b_send, b_recv, o_send, o_recv, l_send, l_recv = rest[11:19]
    a_send, a_recv, s_send, s_recv, z_send, z_recv, x_send, x_recv, p_sem, local_sem = rest[19:]
    seq = lax.axis_index("seq")
    kvh = lax.axis_index("kvh")
    z, x = seq // XN, seq % XN
    y, core = kvh // 2, kvh % 2

    def ahead(shift):
        return ((z + shift // XN) % ZN) * XN + (x + shift % XN) % XN

    def behind(shift):
        return ((z + ZN - shift // XN) % ZN) * XN + (x + XN - shift % XN) % XN

    def chip(step):
        return ((y + step) % YN) * 2 + core

    sibling = y * 2 + 1 - core
    cache = pltpu.make_async_copy(cache_ref, kv_ref, local_sem.at[1 + parts])
    cache.start()

    barrier = pltpu.get_barrier_semaphore()

    def greet_seq(shift, carry):
        pl.semaphore_signal(
            barrier, inc=1, device_id={"seq": ahead(shift)}, device_id_type=MESH
        )
        return carry

    lax.fori_loop(1, SEQ, greet_seq, 0)
    for peer in [chip(1), chip(2), chip(3), sibling]:
        pl.semaphore_signal(barrier, inc=1, device_id={"kvh": peer}, device_id_type=MESH)
    partner = {"seq": kvh * XN + x, "kvh": z}

    @pl.when(kvh != z)
    def _():
        pl.semaphore_signal(barrier, inc=1, device_id=partner, device_id_type=MESH)
        pl.semaphore_wait(barrier, SEQ + YN)

    @pl.when(kvh == z)
    def _():
        pl.semaphore_wait(barrier, SEQ - 1 + YN)

    def remote(src, dst, send, recv, **device):
        return pltpu.make_async_remote_copy(
            src_ref=src,
            dst_ref=dst,
            send_sem=send,
            recv_sem=recv,
            device_id=device,
            device_id_type=MESH,
        )

    def blk_copy(shift):
        return remote(
            blk_ref.at[shift], in_blk.at[shift], b_send.at[shift], b_recv.at[shift], seq=ahead(shift)
        )

    def q_copy(head, shift):
        return remote(
            out_q.at[shift, head],
            in_q.at[shift, head],
            q_send.at[head, shift],
            q_recv.at[head, shift],
            seq=ahead(shift),
        )

    def o_copy(index, shift):
        head, first, count = PARTS[index]
        return remote(
            out_o.at[shift, head, pl.ds(first, count)],
            in_o[index].at[shift],
            o_send.at[index, shift],
            o_recv.at[index, shift],
            seq=behind(shift),
        )

    def l_copy(head, shift):
        return remote(
            out_l[head].at[shift],
            in_l[head].at[shift],
            l_send.at[head, shift],
            l_recv.at[head, shift],
            seq=behind(shift),
        )

    def lanes(group):
        return pl.ds(pl.multiple_of(group * HD, HD), HD)

    def a_copy(index, step):
        return remote(
            own_att[index],
            att[index].at[:, lanes(kvh)],
            a_send.at[index, step],
            a_recv.at[index, step],
            kvh=chip(step),
        )

    def s_copy(index, step):
        part = att[index].at[:, lanes(chip(YN - step))]
        return remote(
            own_att[index] if step == 0 else part,
            part,
            s_send.at[index, step],
            s_recv.at[index, step],
            kvh=sibling,
        )

    def z_copy(way, step):
        block = (z + ZN - step + 1) % ZN if way == 0 else (z + step - 1) % ZN
        part = wbuf.at[x, block]
        return remote(
            part,
            part,
            z_send.at[way, step],
            z_recv.at[way, step],
            seq=((z + 1) % ZN if way == 0 else (z + ZN - 1) % ZN) * XN + x,
        )

    def p_copy():
        return remote(w_ref, wbuf.at[x, kvh], p_sem.at[0], p_sem.at[1], **partner)

    def x_copy(piece, step):
        block = (z + ZN - piece) % ZN
        part = wbuf.at[x, block]
        return remote(
            part,
            part,
            x_send.at[piece, step],
            x_recv.at[piece, step],
            seq=z * XN + (x + step) % XN,
        )

    def x_start(*pieces):
        for piece in pieces:
            for step in (2, 1, 3):
                x_copy(piece, step).start()

    z_steps = (ZN // 2, ZN // 2 - 1)

    def z_start(step):
        for way in range(2):
            if step <= z_steps[way]:
                z_copy(way, step).start()

    def z_wait(step):
        for way in range(2):
            if step <= z_steps[way]:
                z_copy(way, step).wait_recv()

    def place(first, count):
        return lax.broadcasted_iota(jnp.int32, (count, TILE), 1) == (
            first + lax.broadcasted_iota(jnp.int32, (count, TILE), 0)
        )

    def own_piece(tile, carry):
        visible = lax.broadcasted_iota(jnp.int32, (TILE, BLK), 1) <= (
            tile * TILE + lax.broadcasted_iota(jnp.int32, (TILE, BLK), 0)
        )
        for head in range(GROUP):
            out, lse = attend(
                q_ref[tile, :, head * HD : (head + 1) * HD],
                kv_ref[0, BLOCKS - 1],
                kv_ref[1, BLOCKS - 1],
                visible,
            )
            own_o[tile, head] = out
            own_l[tile, head] = to_row(lse, place(0, TILE))
        return carry

    def send_blk(shift, carry):
        blk_copy(shift).start()
        return carry

    def send_queries(head):
        def pack(shift, carry):
            out_q[shift, head] = q_ref[tab[shift], :, head * HD : (head + 1) * HD]
            q_copy(head, shift).start()
            return carry

        in_q[0, head] = q_ref[tab[0], :, head * HD : (head + 1) * HD]
        lax.fori_loop(1, SEQ, pack, 0)

    def serve_head(head, between=()):
        spot = place(0, TILE)
        mine = [n for n, part in enumerate(PARTS) if part[0] == head]

        def serve(shift):
            block = blk_s[shift, 0, 0]
            out, lse = attend(in_q[shift, head], kv_ref[0, block], kv_ref[1, block], None)
            return out, to_row(lse, spot)

        def step(shift, carry):
            q_copy(head, shift).wait_recv()
            out, row = serve(shift)
            out_o[shift, head] = out
            out_l[head][shift] = row
            o_copy(mine[0], shift).start()
            l_copy(head, shift).start()
            return carry

        out, row = serve(0)
        in_l[head][0] = row
        for index in mine:
            _, first, count = PARTS[index]
            in_o[index][0] = out[first : first + count]
        cuts = [1 + (SEQ - 1) * n // (len(between) + 1) for n in range(len(between) + 2)]
        for number in range(len(cuts) - 1):
            lax.fori_loop(cuts[number], cuts[number + 1], step, 0)
            if number < len(between):
                piece, distance = between[number]
                x_copy(piece, distance).start()
        for index in mine[1:]:

            def later(shift, carry, index=index):
                o_copy(index, shift).start()
                return carry

            lax.fori_loop(1, SEQ, later, 0)

    def mix_part(index):
        head, first, count = PARTS[index]
        spot = place(first, count)

        def arrived(shift, carry):
            o_copy(index, shift).wait_recv()
            if first == 0:
                l_copy(head, shift).wait_recv()
            return carry

        lax.fori_loop(1, SEQ, arrived, 0)

        def mix(tile, carry):
            one = tab[SEQ + tile * SEL]
            two = tab[SEQ + tile * SEL + 1]
            rows = [own_l[tile, head], in_l[head][one], in_l[head][two]]
            outs = [
                own_o[tile, head, first : first + count, :],
                in_o[index][one],
                in_o[index][two],
            ]
            high = jnp.maximum(jnp.maximum(rows[0], rows[1]), rows[2])
            shares = [jnp.exp(r - high) for r in rows]
            norm = shares[0] + shares[1] + shares[2]
            blended = jnp.zeros((count, HD), jnp.float32)
            for share, out in zip(shares, outs):
                blended = blended + to_column(share / norm, spot) * out.astype(jnp.float32)
            own_att[index][pl.ds(pl.multiple_of(tile * count, count), count), :] = blended.astype(
                jnp.bfloat16
            )
            return carry

        lax.fori_loop(0, TILES, mix, 0)
        for step in range(1, YN):
            a_copy(index, step).start()
        s_copy(index, 0).start()
        keep(index).start()

    def keep(index):
        return pltpu.make_async_copy(
            own_att[index], att[index].at[:, lanes(kvh)], local_sem.at[1 + index]
        )

    def pass_on(index):
        for step in range(1, YN):
            a_copy(index, step).wait_recv()
            s_copy(index, step).start()

    def project(index):
        head, first, count = PARTS[index]
        for step in range(YN):
            s_copy(index, step).wait_recv()
        keep(index).wait()
        group = 256 // count

        def rows_of(number, carry):
            rows = pl.ds(pl.multiple_of(number * 256, 256), 256)
            term = jnp.dot(
                att[index][rows, :],
                wfull[head * KVN * HD : (head + 1) * KVN * HD, :],
                preferred_element_type=jnp.float32,
            ).reshape(group, count, XN * HD)
            target = (pl.ds(number * group, group), pl.ds(first, count))
            if head > 0:
                term = acc[target] + term
            if head == GROUP - 1:
                out_ref[target] = term.astype(jnp.bfloat16)
            else:
                acc[target] = term
            return carry

        lax.fori_loop(0, TILES // group, rows_of, 0)

    @pl.when(kvh != z)
    def _():
        p_copy().start()

    @pl.when(kvh == z)
    def _():
        wbuf[x, z] = w_ref[...]

    lax.fori_loop(1, SEQ, send_blk, 0)
    tiles = TILES // GROUP
    for index in range(GROUP):
        send_queries(index)
        if index == 0:
            cache.wait()
        if index == 1:
            x_start(0)
        if index == 2:
            x_start(1, 7)
        lax.fori_loop(index * tiles, (index + 1) * tiles, own_piece, 0)
        if index == 0:

            @pl.when(kvh != z)
            def _():
                p_copy().wait()

        else:
            z_wait(index)
        z_start(index + 1)

    def wait_blk(shift, carry):
        blk_copy(shift).wait_recv()
        return carry

    lax.fori_loop(1, SEQ, wait_blk, 0)
    in_blk[0] = blk_ref[0]
    fetch = pltpu.make_async_copy(in_blk, blk_s, local_sem.at[0])
    fetch.start()
    fetch.wait()

    serve_head(0, [(p, d) for p in (2, 6) for d in (2, 1, 3)])
    z_wait(GROUP)
    serve_head(1, [(p, d) for p in (3, 5) for d in (2, 1, 3)])
    serve_head(2, [(4, d) for d in (2, 1, 3)])
    mix_part(0)
    serve_head(3)
    mix_part(1)
    pass_on(0)

    for piece in range(ZN):
        for step in range(1, XN):
            x_copy(piece, step).wait_recv()
    for head in range(GROUP):

        def arrange(group, carry, head=head):
            row = pl.multiple_of((head * KVN + group) * HD, HD)
            for col in range(XN):
                wfull[pl.ds(row, HD), col * HD : (col + 1) * HD] = wbuf[
                    col, group, head * HD : (head + 1) * HD, :
                ]
            return carry

        lax.fori_loop(0, KVN, arrange, 0)

    mix_part(2)
    pass_on(1)
    for index in range(3, parts):
        mix_part(index)
    pass_on(2)
    project(0)
    project(1)
    for index in range(3, parts):
        pass_on(index)
    project(2)
    for index in range(3, parts):
        project(index)

    def finish_q(shift, carry):
        for head in range(GROUP):
            q_copy(head, shift).wait_send()
            l_copy(head, shift).wait_send()
        return carry

    lax.fori_loop(1, SEQ, finish_q, 0)
    for index in range(parts):

        def finish(shift, carry, index=index):
            o_copy(index, shift).wait_send()
            return carry

        lax.fori_loop(1, SEQ, finish, 0)
        for step in range(1, YN):
            a_copy(index, step).wait_send()
        for step in range(YN):
            s_copy(index, step).wait_send()

    def finish_blk(shift, carry):
        blk_copy(shift).wait_send()
        return carry

    lax.fori_loop(1, SEQ, finish_blk, 0)
    for way in range(2):
        for step in range(1, z_steps[way] + 1):
            z_copy(way, step).wait_send()
    for piece in range(ZN):
        for step in range(1, XN):
            x_copy(piece, step).wait_send()


def per_device(queries, kv_cache, selected, out_weight):
    rows = queries.shape[0]
    seq = lax.axis_index("seq")
    z, x = seq // XN, seq % XN
    own_block = seq * BLOCKS + BLOCKS - 1
    chosen = selected.reshape(TILES * SEL)
    target = jnp.where(chosen >= own_block, chosen + 1, chosen)
    holder = target // BLOCKS
    within = target % BLOCKS
    shift = ((holder // XN - z + ZN) % ZN) * XN + (holder % XN - x + XN) % XN
    routing = shift[None, :] == jnp.arange(SEQ, dtype=jnp.int32)[:, None]
    request_tile = jnp.arange(TILES * SEL, dtype=jnp.int32) // SEL
    slot_tile = jnp.sum(jnp.where(routing, request_tile[None, :], 0), axis=1)
    slot_block = jnp.sum(jnp.where(routing, within[None, :], 0), axis=1)
    table = jnp.concatenate([slot_tile, shift]).astype(jnp.int32)
    slot_block = jnp.broadcast_to(slot_block.astype(jnp.int32)[:, None, None], (SEQ, 1, 128))

    parts = len(PARTS)
    vmem = pl.BlockSpec(memory_space=pltpu.VMEM)
    dma = pltpu.SemaphoreType.DMA
    slots = pltpu.VMEM((SEQ, GROUP, TILE, HD), jnp.bfloat16)
    stats = pltpu.VMEM((SEQ, 1, TILE), jnp.float32)
    out = pl.pallas_call(
        fused,
        name="fused",
        out_shape=jax.ShapeDtypeStruct((TILES, TILE, XN * HD), jnp.bfloat16),
        in_specs=[
            pl.BlockSpec(memory_space=pltpu.SMEM),
            vmem,
            pl.BlockSpec(memory_space=pl.ANY),
            vmem,
            vmem,
        ],
        out_specs=vmem,
        scratch_shapes=[pltpu.VMEM((SEQ, n, HD), jnp.bfloat16) for _, _, n in PARTS]
        + [pltpu.VMEM((TILES * n, KVN * HD), jnp.bfloat16) for _, _, n in PARTS]
        + [pltpu.VMEM((TILES * n, HD), jnp.bfloat16) for _, _, n in PARTS]
        + [stats] * (2 * GROUP)
        + [
            slots,
            slots,
            slots,
            pltpu.VMEM((TILES, GROUP, TILE, HD), jnp.bfloat16),
            pltpu.VMEM((TILES, GROUP, 1, TILE), jnp.float32),
            pltpu.VMEM((SEQ, 1, 128), jnp.int32),
            pltpu.SMEM((SEQ, 1, 128), jnp.int32),
            pltpu.VMEM((XN, KVN, GROUP * HD, HD), jnp.bfloat16),
            pltpu.VMEM((KVN * GROUP * HD, XN * HD), jnp.bfloat16),
            pltpu.VMEM((TILES, TILE, XN * HD), jnp.float32),
            pltpu.VMEM((2, BLOCKS, BLK, HD), jnp.bfloat16),
        ]
        + [dma((GROUP, SEQ))] * 2
        + [dma((SEQ,))] * 2
        + [dma((parts, SEQ))] * 2
        + [dma((GROUP, SEQ))] * 2
        + [dma((parts, YN))] * 4
        + [dma((2, ZN))] * 2
        + [dma((ZN, XN))] * 2
        + [dma((2,))]
        + [dma((2 + parts,))],
        compiler_params=pltpu.CompilerParams(
            collective_id=0, has_side_effects=True, vmem_limit_bytes=60 << 20
        ),
    )(
        table,
        queries.reshape(TILES, TILE, GROUP * HD),
        kv_cache.reshape(2, BLOCKS, BLK, HD),
        slot_block,
        out_weight,
    )
    return out.reshape(rows, XN * HD)


def solution(mesh):
    in_specs = (P("seq", "kvh"), P(None, "seq", "kvh"), P("seq", "kvh", None), P("kvh", "seq"))
    out_specs = P("seq", "kvh")
    return jax.shard_map(
        per_device, mesh=mesh, in_specs=in_specs, out_specs=out_specs, check_vma=False
    )
```

time: 248 us -> 243 us (0.980)
  Pallas kernels: 243 us -> 237 us
    pallas_call x1, Pallas kernels: 243 us -> 237 us  [per_device(): pl.pallas_call(fused, name='fused', out_shape=jax.ShapeDtypeStruct((TILES...]
where the time goes in v3:
time: 243 us; the launch traced here: 241 us
  Pallas kernels  237 us (98%)
  local copies, waits for them, and re-layouts  3.8 us (2%)
    pallas_call x1, Pallas kernels, per_device(): pl.pallas_call(fused, name='fused', out_shape=jax.ShapeDtypeStruct((TILES...  237 us

profile of v3, /device:TPU:1, one launch (start us, length us, event | category | flops | bytes accessed | tf_op | source)
XLA Modules:
  0.0 241.2 jit_solution(3605404003100650495)
XLA Ops:
  0.0 0.8 copy.7
  0.8 0.1 reshape.128
  0.9 0.1 select_reduce_fusion
  1.0 0.7 pad_add_fusion.tab
  1.6 0.7 broadcast_in_dim.31.blk_ref
  2.3 236.5 %fused.1 = bf16[8,128,512]{2,1,0:T(8,128)(2,1)} custom-call(s32[48]{0:T(128)} %pad_add_fusion.tab, bf16[8,128,512]{2,1,0:T(8,128)(2,1)} %bitcast.7, bf16[2,8,1024,128]{3,2,1,0:T(8,128)(2,1)} %bitcast.6, s32[32,1,128]{2,1,0:T(1,128)} %broadcast_in_dim.31.blk_ref, bf16[512,128]{1,0:T(8,128)(2,1)} %w_ref.1), custom_call_target="tpu_custom_call" | custom-call | tf_op jit(solution)/shard_map/fused/pallas_call | solution.py:479
  238.9 2.3 copy.9
  (2 shorter events, 0.0 us)

commit v4 on v3

--- a/solution.py
+++ b/solution.py
@@ -306,7 +306,7 @@
             return carry
 
         lax.fori_loop(0, TILES, mix, 0)
-        for step in range(1, YN):
+        for step in (2, 1, 3):
             a_copy(index, step).start()
         s_copy(index, 0).start()
         keep(index).start()
@@ -317,7 +317,7 @@
         )
 
     def pass_on(index):
-        for step in range(1, YN):
+        for step in (1, 3, 2):
             a_copy(index, step).wait_recv()
             s_copy(index, step).start()
 
@@ -414,9 +414,10 @@
     for index in range(3, parts):
         mix_part(index)
     pass_on(2)
+    pass_on(3)
     project(0)
     project(1)
-    for index in range(3, parts):
+    for index in range(4, parts):
         pass_on(index)
     project(2)
     for index in range(3, parts):

time: 243 us -> 244 us (level)
  no operation moved by 1% of the time
where the time goes in v4:
time: 244 us; the launch traced here: 241 us
  Pallas kernels  236 us (97%)
  local copies, waits for them, and re-layouts  3.8 us (2%)
    pallas_call x1, Pallas kernels, per_device(): pl.pallas_call(fused, name='fused', out_shape=jax.ShapeDtypeStruct((TILES...  236 us

profile of v4, /device:TPU:1, one launch (start us, length us, event | category | flops | bytes accessed | tf_op | source)
XLA Modules:
  0.0 240.7 jit_solution(272915770352846842)
XLA Ops:
  0.0 0.8 copy.7
  0.8 0.1 reshape.128
  0.9 0.1 select_reduce_fusion
  1.0 0.7 pad_add_fusion.tab
  1.6 0.7 broadcast_in_dim.31.blk_ref
  2.3 236.0 %fused.1 = bf16[8,128,512]{2,1,0:T(8,128)(2,1)} custom-call(s32[48]{0:T(128)} %pad_add_fusion.tab, bf16[8,128,512]{2,1,0:T(8,128)(2,1)} %bitcast.7, bf16[2,8,1024,128]{3,2,1,0:T(8,128)(2,1)} %bitcast.6, s32[32,1,128]{2,1,0:T(1,128)} %broadcast_in_dim.31.blk_ref, bf16[512,128]{1,0:T(8,128)(2,1)} %w_ref.1), custom_call_target="tpu_custom_call" | custom-call | tf_op jit(solution)/shard_map/fused/pallas_call | solution.py:480
  238.4 2.3 copy.9
  (2 shorter events, 0.0 us)
